TPU v7x, 32 devices: a whole 2x2x4 slice. The times are simulated.
32 devices in a mesh: seq: 8 (over z, y), head: 4 (over x, core).
Axes of the slice: x: 2, y: 2, z: 4, core: 2. Of those that a mesh axis runs over, the one named last changes fastest.
Arguments:
- query: bfloat16 [4096, 1024], P('seq', 'head'), may hold values from -70 to 70
- key: bfloat16 [4096, 1024], P('seq', 'head'), may hold values from -15 to 15
- value: bfloat16 [4096, 1024], P('seq', 'head'), may hold values from -6 to 6
- middle_offsets: int32 [16], P('head'), may hold values from 0 to 3
- upper_offsets: int32 [16], P('head'), may hold values from 0 to 3
- out_weight: bfloat16 [1024, 1024], P('head'), may hold values from -0.1875 to 0.1875
Outputs:
- projected: bfloat16 [4096, 1024], P(('seq', 'head'))
All inputs are finite; a program needn't handle non-finite values.
Results may differ from a plain program's by a relative error of at most 0.0051.
Values may be sent and summed in bfloat16 or wider, within the bound.
A program may use at most 64 MiB of HBM per device.

v0:
```python
import jax
import jax.numpy as jnp
from jax import lax
from jax.sharding import PartitionSpec as P

HD = 64
SPAN = 8
MIDDLE_DILATION = 4


def partner_2(value, axis, stride):
    mask = 2**stride
    pairs = [(source, source ^ mask) for source in range(lax.axis_size(axis))]
    return lax.ppermute(value, axis, pairs)


def attend_segment(query_matrix_rows, key_matrix_rows, value_matrix_rows):
    scores = jnp.einsum(
        "qhd,khd->hqk", query_matrix_rows, key_matrix_rows, preferred_element_type=jnp.float32
    ) * HD ** (-0.5)
    row_max = jnp.max(scores, axis=2)
    mass = jnp.exp(scores - row_max[:, :, None])
    total = jnp.sum(mass, axis=2)
    soft_weights = mass.astype(jnp.bfloat16)
    weighted = jnp.einsum(
        "hqk,khd->qhd", soft_weights, value_matrix_rows, preferred_element_type=jnp.float32
    )
    return (weighted, total.T, row_max.T)


def attend_blocks(query_matrix_rows, key_matrix_rows, value_matrix_rows):
    block_size = min(512, query_matrix_rows.shape[0])
    pieces = query_matrix_rows.reshape(
        query_matrix_rows.shape[0] // block_size,
        block_size,
        query_matrix_rows.shape[1],
        query_matrix_rows.shape[2],
    )

    def one_block(one_piece):
        return attend_segment(one_piece, key_matrix_rows, value_matrix_rows)

    weighted, total, row_max = lax.map(one_block, pieces)
    return (
        weighted.reshape(query_matrix_rows.shape),
        total.reshape(query_matrix_rows.shape[:2]),
        row_max.reshape(query_matrix_rows.shape[:2]),
    )


def picked_rows(block_rows, offsets, stride):
    group_count = block_rows.shape[0] // stride
    grouped = block_rows.reshape(group_count, stride, block_rows.shape[1], block_rows.shape[2])
    chosen = (
        jnp.arange(stride, dtype=jnp.int32)[None, :, None, None] == offsets[None, None, :, None]
    )
    return jnp.sum(jnp.where(chosen, grouped, jnp.zeros((), grouped.dtype)), axis=1)


def scatter_rows(values, offsets, stride, filler):
    chosen = jnp.arange(stride, dtype=jnp.int32)[:, None] == offsets[None, :]
    spread_out = jnp.where(chosen[None], values[:, None], filler)
    return spread_out.reshape((values.shape[0] * stride,) + values.shape[1:])


def flatten_level(result):
    row_total = result[0].shape[0]
    weighted = result[0].reshape(row_total, -1)
    total = jnp.repeat(result[1], HD, axis=1)
    row_max = jnp.repeat(result[2], HD, axis=1)
    return (weighted, total, row_max)


def scatter_level(result, offsets, stride):
    weighted, total, row_max = flatten_level(result)
    column_offsets = jnp.repeat(offsets, HD)
    return (
        scatter_rows(weighted, column_offsets, stride, 0.0),
        scatter_rows(total, column_offsets, stride, 0.0),
        scatter_rows(row_max, column_offsets, stride, -jnp.inf),
    )


def combine(levels):
    highest = levels[0][2]
    for one_level in levels[1:]:
        highest = jnp.maximum(highest, one_level[2])
    numerator = jnp.zeros(levels[0][0].shape, jnp.float32)
    denominator = jnp.zeros(levels[0][1].shape, jnp.float32)
    for one_level in levels:
        factor = jnp.exp(one_level[2] - highest)
        numerator = numerator + factor * one_level[0]
        denominator = denominator + factor * one_level[1]
    return (numerator / denominator).astype(jnp.bfloat16)


def per_device(query, key, value, middle_offsets, upper_offsets, out_weight):
    row_count = query.shape[0]
    head_count = query.shape[1] // HD
    top_stride = lax.axis_size("seq") // 2
    query_matrix_rows = query.reshape(row_count, head_count, HD)
    key_matrix_rows = key.reshape(row_count, head_count, HD)
    value_matrix_rows = value.reshape(row_count, head_count, HD)
    top_key_local = picked_rows(key_matrix_rows, upper_offsets, top_stride).reshape(
        -1, head_count * HD
    )
    top_value_local = picked_rows(value_matrix_rows, upper_offsets, top_stride).reshape(
        -1, head_count * HD
    )
    top_key_all, top_value_all = (
        lax.all_gather(top_key_local, "seq", axis=0, tiled=True),
        lax.all_gather(top_value_local, "seq", axis=0, tiled=True),
    )
    upper_level = attend_segment(
        picked_rows(query_matrix_rows, upper_offsets, top_stride),
        top_key_all.reshape(-1, head_count, HD),
        top_value_all.reshape(-1, head_count, HD),
    )
    middle_pair = jnp.stack(
        [
            picked_rows(key_matrix_rows, middle_offsets, MIDDLE_DILATION),
            picked_rows(value_matrix_rows, middle_offsets, MIDDLE_DILATION),
        ]
    ).reshape(2, -1, head_count * HD)
    for bit_number in range(SPAN.bit_length() - 1):
        partner = partner_2(middle_pair, "seq", bit_number)
        middle_pair = jnp.concatenate([middle_pair, partner], axis=1)
    middle_level = attend_segment(
        picked_rows(query_matrix_rows, middle_offsets, MIDDLE_DILATION),
        middle_pair[0].reshape(-1, head_count, HD),
        middle_pair[1].reshape(-1, head_count, HD),
    )
    bottom = flatten_level(attend_blocks(query_matrix_rows, key_matrix_rows, value_matrix_rows))
    attention = combine(
        (
            bottom,
            scatter_level(middle_level, middle_offsets, MIDDLE_DILATION),
            scatter_level(upper_level, upper_offsets, top_stride),
        )
    )
    summed = lax.psum_scatter(
        jnp.dot(attention, out_weight, preferred_element_type=jnp.float32),
        "head",
        scatter_dimension=0,
        tiled=True,
    )
    return summed.astype(jnp.bfloat16)


def solution(mesh):
    in_specs = (
        P("seq", "head"),
        P("seq", "head"),
        P("seq", "head"),
        P("head"),
        P("head"),
        P("head", None),
    )
    out_specs = P(("seq", "head"), None)
    return jax.shard_map(
        per_device, mesh=mesh, in_specs=in_specs, out_specs=out_specs, check_vma=False
    )
```

profile of v0, /device:TPU:0, one launch (start us, length us, event | category | flops | bytes accessed | tf_op | source)
XLA Modules:
  0.0 164.0 jit_solution(4376389824751921904)
XLA Ops:
  6.5 1.3 reshape_reshape.16
  7.8 1.2 reshape_reshape.17
  9.1 0.0 copy-start.5
  9.1 0.0 copy-start.6
  9.1 1.3 reshape_reshape.18
  10.4 0.0 copy-done.8
  10.4 0.0 copy-done.9
  10.4 2.6 %select_reduce_fusion.4 = (bf16[128,4,64]{2,1,0:T(4,128)(2,1)S(1)}, bf16[128,4,64]{2,1,0:T(4,128)(2,1)S(1)}, bf16[128,4,64]{2,1,0:T(4,128)(2,1)S(1)}, bf16[128,4...) fusion(bf16[128,4,4,64]{3,2,1,0:T(4,128)(2,1)S(1)} %reshape_reshape.17, ...), kind=kLoop, calls=%fused_computation.41 | loop fusion | flops 1376256 | bytes 1179680 | tf_op jit(solution)/shard_map/reduce_sum | solution.py:57
  13.1 0.1 copy.65
  13.2 0.1 copy.66
  13.4 3.0 %collective-permute-start = (bf16[2,128,256]{1,2,0:T(8,128)(2,1)S(1)}, bf16[2,128,256]{1,2,0:T(8,128)(2,1)S(1)}, u32[]{:S(2)}, u32[]{:S(2)}) collective-permute-start(bf16[2,128,256]{1,2,0:T(8,128)(2,1)S(1)} %pad_maximum_fusion.3), channel_id=1, source_target_pairs={{0,4},{4,0},{8,12},{12,8},{16,20},{20,16},{24,28},{28,24},{1,5},{5... | collective-permute-start | bytes 393224 | tf_op jit(solution)/shard_map/ppermute | solution.py:14
  16.4 0.1 copy.63
  16.5 0.1 copy.64
  16.7 0.1 copy.70
  16.8 28.2 %all_gather.6 = bf16[1024,256]{0,1:T(8,128)(2,1)S(1)} all-gather(bf16[128,256]{0,1:T(8,128)(2,1)S(1)} %bitcast.102), channel_id=1, replica_groups=mesh['seq'=8,'head'=4] {'seq'}, dimensions={0}, use_global_device_ids=true | all-gather | bytes 589824 | tf_op jit(solution)/shard_map/all_gather | solution.py:111
  45.0 0.1 copy.80
  45.1 27.4 %all_gather.7 = bf16[1024,256]{0,1:T(8,128)(2,1)S(1)} all-gather(bf16[128,256]{0,1:T(8,128)(2,1)S(1)} %bitcast.103), channel_id=1, replica_groups=mesh['seq'=8,'head'=4] {'seq'}, dimensions={0}, use_global_device_ids=true | all-gather | bytes 589824 | tf_op jit(solution)/shard_map/all_gather | solution.py:112
  72.6 0.5 multiply_reduce_fusion.1
  73.1 0.5 fusion.8
  73.6 0.6 fusion.10
  74.2 0.1 copy.81
  74.3 0.1 copy.85
  74.4 0.1 copy.72
  74.5 0.1 broadcast_in_dim.185
  74.6 0.1 eq.54
  74.7 2.7 %multiply_reduce_fusion = (f32[4,512]{1,0:T(4,128)S(1)}, f32[4,512,512]{1,2,0:T(8,128)}) fusion(bf16[512,4,64]{0,2,1:T(8,128)(2,1)S(1)} %bitcast.94, bf16[512,4,64]{0,2,1:T(8,128)(2,1)S(1)} %bitcast.95), kind=kOutput, calls=%fused_computation.1 | convolution fusion | flops 136312832 | bytes 4726784 | tf_op jit(solution)/shard_map/while/body/eval_jaxpr/qhd,khd->hqk/dot_general | solution.py:18
  77.4 0.4 broadcast_select_fusion.4
  77.7 0.6 copy-done.7
  78.3 0.1 copy.74
  78.4 0.1 broadcast_in_dim.177
  78.5 0.1 eq.47
  78.6 0.2 select_n.70
  78.8 1.0 copy.73
  79.8 0.2 select_n.75
  80.0 1.0 copy.82
  81.0 0.2 select_n.79
  81.2 1.0 copy.86
  82.2 0.0 collective-permute-done
  82.2 0.5 collective-permute-start.1
  82.7 3.0 %fusion = f32[4,512]{1,0:T(4,128)S(1)} fusion(f32[4,512,512]{1,2,0:T(8,128)} %get-tuple-element.49, f32[4,512]{1,0:T(4,128)S(1)} %get-tuple-element.48), kind=kLoop, calls=%fused_computation.2 | loop fusion | flops 3143680 | bytes 4210688 | tf_op jit(solution)/shard_map/while/body/eval_jaxpr/reduce_sum | solution.py:23
  85.8 8.4 %collective-permute-done.1 = bf16[2,256,256]{1,2,0:T(8,128)(2,1)S(1)} collective-permute-done((bf16[2,256,256]{1,2,0:T(8,128)(2,1)S(1)}, bf16[2,256,256]{1,2,0:T(8,128)(2,1)S(1)}, u32[]{:S(2)}, u32[]{:S(2)}) %collective-permute-start.1) | collective-permute-done | bytes 262176 | tf_op jit(solution)/shard_map/ppermute | solution.py:14
  94.2 0.1 collective-permute-start.2
  94.3 0.8 fusion.2
  95.2 13.8 %collective-permute-done.2 = bf16[2,512,256]{1,2,0:T(8,128)(2,1)S(1)} collective-permute-done((bf16[2,512,256]{1,2,0:T(8,128)(2,1)S(1)}, bf16[2,512,256]{1,2,0:T(8,128)(2,1)S(1)}, u32[]{:S(2)}, u32[]{:S(2)}) %collective-permute-start.2) | collective-permute-done | bytes 524320 | tf_op jit(solution)/shard_map/ppermute | solution.py:14
  109.0 0.1 pad_maximum_fusion
  109.1 0.9 fusion.36
  110.0 0.5 multiply_reduce_fusion.2
  110.5 0.5 fusion.6
  111.0 0.1 copy.83
  111.1 1.6 fusion.12
  112.7 0.1 copy.77
  112.8 0.1 copy.68
  112.9 1.4 broadcast_select_fusion.5
  114.3 0.2 select_n.66
  114.5 0.2 copy.69
  114.7 2.2 %select_n.72 = f32[512,256]{1,0:T(8,128)} reshape(f32[128,4,256]{2,1,0:T(4,128)} %get-tuple-element.39) | data formatting | bytes 1048576 | tf_op jit(solution)/shard_map/jit(_where)/select_n | solution.py:62
  116.9 2.0 %copy.78 = f32[512,256]{0,1:T(8,128)} copy(f32[512,256]{1,0:T(8,128)} %select_n.72) | data formatting | bytes 1048576 | tf_op jit(solution)/shard_map/jit(_where)/select_n | solution.py:62
  118.9 2.0 %select_n.77 = f32[512,256]{1,0:T(8,128)} reshape(f32[128,4,256]{2,1,0:T(4,128)} %get-tuple-element.40) | data formatting | bytes 1048576 | tf_op jit(solution)/shard_map/jit(_where)/select_n | solution.py:62
  120.9 2.1 %copy.84 = f32[512,256]{0,1:T(8,128)} copy(f32[512,256]{1,0:T(8,128)} %select_n.77) | data formatting | bytes 1048576 | tf_op jit(solution)/shard_map/jit(_where)/select_n | solution.py:62
  123.0 1.6 fusion.28
  124.6 1.8 %fusion.37 = f32[512,1024]{1,0:T(8,128)} fusion(bf16[512,256]{0,1:T(8,128)(2,1)S(1)} %fusion.28, bf16[256,1024]{1,0:T(8,128)(2,1)S(1)} %copy-done), kind=kOutput, calls=%fused_computation.64 | convolution fusion | flops 268435456 | bytes 2883584 | tf_op jit(solution)/shard_map/dot_general | solution.py:142
  126.5 0.0 reduce-scatter.2.cloned.1.call-update
  126.5 28.9 %reduce-scatter.2.cloned.1.call-done = f32[128,1024]{1,0:T(8,128)} async-done(((f32[512,1024]{1,0:T(8,128)}), f32[128,1024]{1,0:T(8,128)}) %reduce-scatter.2.cloned.1.call-update) | async-done | bytes 524304 | tf_op jit(solution)/shard_map/reduce_scatter | solution.py:141
  155.4 1.8 %convert_element_type.16 = bf16[128,1024]{1,0:T(8,128)(2,1)} convert(f32[128,1024]{1,0:T(8,128)} %reduce-scatter.2.cloned.1.call-done) | non-fusion elementwise | flops 131072 | bytes 786432 | tf_op jit(solution)/shard_map/convert_element_type | solution.py:147
  (26 shorter events, 0.2 us)
Async XLA Ops:
  6.5 118.1 %copy-start = (bf16[256,1024]{1,0:T(8,128)(2,1)S(1)}, bf16[256,1024]{1,0:T(8,128)(2,1)}, u32[]{:S(2)}) copy-start(bf16[256,1024]{1,0:T(8,128)(2,1)} %param.11) | copy-start | bytes 1572868
  6.5 3.9 %copy-start.8 = (s32[4]{0:T(128)S(1)}, s32[4]{0:T(128)}, u32[]{:S(2)}) copy-start(s32[4]{0:T(128)} %param.10) | copy-start | bytes 52
  6.5 3.9 %copy-start.9 = (s32[4]{0:T(128)S(1)}, s32[4]{0:T(128)}, u32[]{:S(2)}) copy-start(s32[4]{0:T(128)} %param.9) | copy-start | bytes 52
  6.5 148.9 %reduce-scatter.2.cloned.1.call-start = ((), (), s32[]{:S(2)}) async-start(), calls=%async_computation.1 | async-start | bytes 2621440 | tf_op jit(solution)/shard_map/reduce_scatter | solution.py:141
  9.1 7.3 %copy-start.5 = (bf16[512,256]{1,0:T(8,128)(2,1)S(1)}, bf16[512,256]{1,0:T(8,128)(2,1)}, u32[]{:S(2)}) copy-start(bf16[512,256]{1,0:T(8,128)(2,1)} %param.6) | copy-start | bytes 786436
  9.1 7.4 %copy-start.6 = (bf16[512,256]{1,0:T(8,128)(2,1)S(1)}, bf16[512,256]{1,0:T(8,128)(2,1)}, u32[]{:S(2)}) copy-start(bf16[512,256]{1,0:T(8,128)(2,1)} %param.7) | copy-start | bytes 786436
  13.4 68.8 %collective-permute-start = (bf16[2,128,256]{1,2,0:T(8,128)(2,1)S(1)}, bf16[2,128,256]{1,2,0:T(8,128)(2,1)S(1)}, u32[]{:S(2)}, u32[]{:S(2)}) collective-permute-start(bf16[2,128,256]{1,2,0:T(8,128)(2,1)S(1)} %pad_maximum_fusion.3), channel_id=1, source_target_pairs={{0,4},{4,0},{8,12},{12,8},{16,20},{20,16},{24,28},{28,24},{1,5},{5... | collective-permute-start | bytes 393224 | tf_op jit(solution)/shard_map/ppermute | solution.py:14
  77.4 0.9 copy-start.7
  82.2 12.0 %collective-permute-start.1 = (bf16[2,256,256]{1,2,0:T(8,128)(2,1)S(1)}, bf16[2,256,256]{1,2,0:T(8,128)(2,1)S(1)}, u32[]{:S(2)}, u32[]{:S(2)}) collective-permute-start(bf16[2,256,256]{1,2,0:T(8,128)(2,1)S(1)} %pad_maximum_fusion.2), channel_id=1, source_target_pairs={{0,8},{4,12},{8,0},{12,4},{16,24},{20,28},{24,16},{28,20},{1,9},{5... | collective-permute-start | bytes 786440 | tf_op jit(solution)/shard_map/ppermute | solution.py:14
  82.7 11.6 %copy-start.1 = (f32[4,512,512]{1,2,0:T(8,128)S(1)}, f32[4,512,512]{1,2,0:T(8,128)}, u32[]{:S(2)}) copy-start(f32[4,512,512]{1,2,0:T(8,128)} %get-tuple-element.49) | copy-start | bytes 12582916
  94.2 14.7 %collective-permute-start.2 = (bf16[2,512,256]{1,2,0:T(8,128)(2,1)S(1)}, bf16[2,512,256]{1,2,0:T(8,128)(2,1)S(1)}, u32[]{:S(2)}, u32[]{:S(2)}) collective-permute-start(bf16[2,512,256]{1,2,0:T(8,128)(2,1)S(1)} %pad_maximum_fusion.1), channel_id=1, source_target_pairs={{0,16},{4,20},{8,24},{12,28},{16,0},{20,4},{24,8},{28,12},{1,17},{... | collective-permute-start | bytes 1572872 | tf_op jit(solution)/shard_map/ppermute | solution.py:14
  114.7 8.3 %copy-start.2 = (f32[512,256]{0,1:T(8,128)S(1)}, f32[512,256]{0,1:T(8,128)}, u32[]{:S(2)}) copy-start(f32[512,256]{0,1:T(8,128)} %copy.73) | copy-start | bytes 1572868
  114.7 8.3 %copy-start.3 = (f32[512,256]{0,1:T(8,128)S(1)}, f32[512,256]{0,1:T(8,128)}, u32[]{:S(2)}) copy-start(f32[512,256]{0,1:T(8,128)} %copy.82) | copy-start | bytes 1572868
  114.7 8.3 %copy-start.4 = (f32[512,256]{0,1:T(8,128)S(1)}, f32[512,256]{0,1:T(8,128)}, u32[]{:S(2)}) copy-start(f32[512,256]{0,1:T(8,128)} %copy.86) | copy-start | bytes 1572868
Sparse Core Ops, SparseCore 0:
  126.6 28.7 reduce-scatter.1
where the time goes:
time: 165 us; the launch traced here: 164 us
  blocking collectives  55.6 us (34%)
  waiting for transfers between devices  51.2 us (31%)
  local copies, waits for them, and re-layouts  19.3 us (12%)
  between operations  13.7 us (8%)
  other arithmetic  12.1 us (7%)
  matrix products  8.54 us (5%)
  starting transfers between devices  3.61 us (2%)
    reduce_scatter x1, waiting for transfers between devices, per_device(): lax.psum_scatter(jnp.dot(attention, out_weight, preferred_element_type=jn...  28.9 us
    all_gather x1, blocking collectives, per_device(): lax.all_gather(top_key_local, 'seq', axis=0, tiled=True)  28.2 us
    all_gather x1, blocking collectives, per_device(): lax.all_gather(top_value_local, 'seq', axis=0, tiled=True)  27.4 us
    ppermute x3, waiting for transfers between devices, partner_2(): return lax.ppermute(value, axis, pairs)  22.2 us
    select_n x12, local copies, waits for them, and re-layouts, scatter_rows(): spread_out = jnp.where(chosen[None], values[:, None], filler)  12.2 us
    reduce_sum x3, other arithmetic, attend_segment(): total = jnp.sum(mass, axis=2)  4.04 us
    another operation x3, local copies, waits for them, and re-layouts, picked_rows(): block_rows.reshape(group_count, stride, block_rows.shape[1], block_rows.s...  3.82 us
    dot_general x3, matrix products, attend_segment(): jnp.einsum('qhd,khd->hqk', query_matrix_rows, key_matrix_rows, preferred_...  3.67 us
  transfers between devices with their start and end apart: 4, of which 3 were waited for; matrix products, arithmetic and copies ran while one was open for 8% of the time, Pallas kernels for 0%

commit v1 on v0

--- a/solution.py
+++ b/solution.py
@@ -1,6 +1,10 @@
+import functools
+
 import jax
 import jax.numpy as jnp
 from jax import lax
+from jax.experimental import pallas as pl
+from jax.experimental.pallas import tpu as pltpu
 from jax.sharding import PartitionSpec as P
 
 HD = 64
@@ -147,6 +151,297 @@
     return summed.astype(jnp.bfloat16)
 
 
+MESH = pl.DeviceIdType.MESH
+STAT_ROWS = 16
+
+
+def dot_f32(left, right):
+    return jnp.dot(left, right, preferred_element_type=jnp.float32)
+
+
+def three_parts(value):
+    high = value.astype(jnp.bfloat16).astype(jnp.float32)
+    rest = value - high
+    middle = rest.astype(jnp.bfloat16).astype(jnp.float32)
+    return [high, middle, rest - middle]
+
+
+def fused_kernel(
+    seq_total,
+    query_ref,
+    key_ref,
+    value_ref,
+    middle_ref,
+    upper_ref,
+    weight_ref,
+    out_ref,
+    select,
+    message,
+    got,
+    result,
+    returned,
+    bottom,
+    bottom_stats,
+    columns,
+    columns_got,
+    weights_got,
+    send_pick,
+    recv_pick,
+    send_back,
+    recv_back,
+    send_columns,
+    recv_columns,
+    send_weight,
+    recv_weight,
+):
+    seq, head = lax.axis_index("seq"), lax.axis_index("head")
+    chip, core = lax.div(head, 2), lax.rem(head, 2)
+    peers = [
+        head,
+        2 * chip + (1 - core),
+        2 * (1 - chip) + core,
+        2 * (1 - chip) + (1 - core),
+    ]
+    rows = query_ref.shape[0]
+    heads = query_ref.shape[1] // HD
+    taken = rows // MIDDLE_DILATION
+    offset_refs = (middle_ref, upper_ref)
+
+    barrier = pltpu.get_barrier_semaphore()
+    for step in range(1, seq_total):
+        pl.semaphore_signal(
+            barrier,
+            inc=1,
+            device_id=(lax.rem(seq + step, seq_total), head),
+            device_id_type=MESH,
+        )
+    for step in range(1, 4):
+        pl.semaphore_signal(
+            barrier, inc=1, device_id=(seq, peers[step]), device_id_type=MESH
+        )
+
+    query_t = (query_ref[...] * jnp.bfloat16(HD**-0.5)).T
+    value_t = value_ref[...].T
+    distance = lax.broadcasted_iota(jnp.int32, (taken, rows), 1) - MIDDLE_DILATION * (
+        lax.broadcasted_iota(jnp.int32, (taken, rows), 0)
+    )
+    for level in range(2):
+        for one in range(heads):
+            pair = level * heads + one
+            span = slice(one * HD, (one + 1) * HD)
+            chosen = jnp.where(
+                distance == offset_refs[level][one], jnp.float32(1), jnp.float32(0)
+            ).astype(jnp.bfloat16)
+            select[pair] = chosen
+            both_t = jnp.concatenate([query_t[span], value_t[span]], axis=0)
+            message[pair, 0 : 2 * HD] = lax.dot_general(
+                both_t,
+                chosen,
+                (((1,), (1,)), ((), ())),
+                preferred_element_type=jnp.float32,
+            ).astype(jnp.bfloat16)
+            picked = dot_f32(chosen, key_ref[:, span])
+            message[pair, 2 * HD : 3 * HD] = jnp.concatenate(
+                [picked[: taken // 2], picked[taken // 2 :]], axis=1
+            ).astype(jnp.bfloat16)
+
+    pl.semaphore_wait(barrier, seq_total + 2)
+    picks = []
+    for step in range(1, seq_total):
+        target = lax.rem(seq + step, seq_total)
+        picks.append(
+            pltpu.make_async_remote_copy(
+                src_ref=message.at[target],
+                dst_ref=got.at[step],
+                send_sem=send_pick.at[step],
+                recv_sem=recv_pick.at[step],
+                device_id=(target, head),
+                device_id_type=MESH,
+            )
+        )
+        picks[-1].start()
+    got[0] = message[seq]
+
+    def weight_copy(source, slot, peer):
+        return pltpu.make_async_remote_copy(
+            src_ref=source,
+            dst_ref=weights_got.at[slot],
+            send_sem=send_weight.at[slot],
+            recv_sem=recv_weight.at[slot],
+            device_id=(seq, peers[peer]),
+            device_id_type=MESH,
+        )
+
+    across = weight_copy(weight_ref, 2, 2)
+    across.start()
+    beside = weight_copy(weight_ref, 1, 1)
+    beside.start()
+
+    half = rows // 2
+    for one in range(heads):
+        span = slice(one * HD, (one + 1) * HD)
+        for part in range(2):
+            lanes = slice(part * half, (part + 1) * half)
+            scores = dot_f32(key_ref[:, span], query_t[span, lanes])
+            row_max = jnp.max(scores, axis=0, keepdims=True)
+            mass = jnp.exp(scores - row_max)
+            bottom_stats[one, 0:1, lanes] = row_max
+            bottom_stats[one, 1:2, lanes] = jnp.sum(mass, axis=0, keepdims=True)
+            bottom[one, :, lanes] = dot_f32(value_t[span], mass.astype(jnp.bfloat16))
+
+    for copy in picks:
+        copy.wait_recv()
+    keys = jnp.concatenate([got[i, 2 * HD : 3 * HD] for i in range(seq_total)], axis=0)
+    values_t = jnp.concatenate([got[i, HD : 2 * HD] for i in range(seq_total)], axis=1)
+    backs = []
+    for part in range(seq_total // 2):
+        block = jnp.concatenate(
+            [got[2 * part, 0:HD], got[2 * part + 1, 0:HD]], axis=1
+        )
+        blank = jnp.zeros_like(block)
+        first = dot_f32(keys, jnp.concatenate([block, blank], axis=0))
+        second = dot_f32(keys, jnp.concatenate([blank, block], axis=0))
+        row_max = jnp.maximum(
+            jnp.max(first, axis=0, keepdims=True), jnp.max(second, axis=0, keepdims=True)
+        )
+        first = jnp.exp(first - row_max)
+        second = jnp.exp(second - row_max)
+        total = jnp.sum(first, axis=0, keepdims=True) + jnp.sum(
+            second, axis=0, keepdims=True
+        )
+        first = first.astype(jnp.bfloat16)
+        second = second.astype(jnp.bfloat16)
+        pieces = []
+        for i in range(seq_total):
+            pieces.append(first[i * HD : (i + 1) * HD])
+            pieces.append(second[i * HD : (i + 1) * HD])
+        weighted = dot_f32(values_t, jnp.concatenate(pieces, axis=0))
+        stats = three_parts(row_max) + three_parts(total)
+        stats.append(jnp.zeros((STAT_ROWS - len(stats), 2 * taken), jnp.float32))
+        packed = jnp.concatenate([weighted] + stats, axis=0).astype(jnp.bfloat16)
+        for step in (2 * part, 2 * part + 1):
+            begin = (step - 2 * part) * taken
+            result[step] = packed[:, begin : begin + taken]
+            if step == 0:
+                returned[seq] = packed[:, begin : begin + taken]
+                continue
+            backs.append(
+                pltpu.make_async_remote_copy(
+                    src_ref=result.at[step],
+                    dst_ref=returned.at[seq],
+                    send_sem=send_back.at[step],
+                    recv_sem=recv_back.at[step],
+                    device_id=(lax.rem(seq - step + seq_total, seq_total), head),
+                    device_id_type=MESH,
+                )
+            )
+            backs[-1].start()
+
+    across.wait_recv()
+    onward = weight_copy(weights_got.at[2], 3, 1)
+    onward.start()
+
+    for step in range(1, seq_total):
+        pltpu.make_async_remote_copy(
+            src_ref=result.at[step],
+            dst_ref=returned.at[lax.rem(seq + step, seq_total)],
+            send_sem=send_back.at[step],
+            recv_sem=recv_back.at[step],
+            device_id=(lax.rem(seq + step, seq_total), head),
+            device_id_type=MESH,
+        ).wait_recv()
+    residue = lax.rem(lax.broadcasted_iota(jnp.int32, (1, rows), 1), MIDDLE_DILATION)
+    for one in range(heads):
+        maxima = [bottom_stats[one, 0:1]]
+        totals = [bottom_stats[one, 1:2]]
+        sums = [bottom[one]]
+        for level in range(2):
+            pair = level * heads + one
+            spread = dot_f32(returned[pair], select[pair])
+            row_max = spread[HD : HD + 1] + spread[HD + 1 : HD + 2] + spread[HD + 2 : HD + 3]
+            maxima.append(
+                jnp.where(residue == offset_refs[level][one], row_max, -jnp.inf)
+            )
+            totals.append(
+                spread[HD + 3 : HD + 4] + spread[HD + 4 : HD + 5] + spread[HD + 5 : HD + 6]
+            )
+            sums.append(spread[0:HD])
+        highest = jnp.maximum(jnp.maximum(maxima[0], maxima[1]), maxima[2])
+        factors = [jnp.exp(row_max - highest) for row_max in maxima]
+        denominator = sum(f * t for f, t in zip(factors, totals))
+        inverse = 1.0 / denominator
+        attention = sum((f * inverse) * w for f, w in zip(factors, sums)).astype(
+            jnp.bfloat16
+        )
+        for i in range(4):
+            columns[i, one * HD : (one + 1) * HD] = attention[
+                :, i * taken : (i + 1) * taken
+            ]
+
+    sent = []
+    for step in range(1, 4):
+        sent.append(
+            pltpu.make_async_remote_copy(
+                src_ref=columns.at[peers[step]],
+                dst_ref=columns_got.at[step],
+                send_sem=send_columns.at[step],
+                recv_sem=recv_columns.at[step],
+                device_id=(seq, peers[step]),
+                device_id_type=MESH,
+            )
+        )
+        sent[-1].start()
+    projected = dot_f32(columns[head].T, weight_ref[...])
+    for step, weight in ((1, beside), (2, None), (3, onward)):
+        if weight is not None:
+            weight.wait_recv()
+        sent[step - 1].wait_recv()
+        projected += dot_f32(columns_got[step].T, weights_got[step])
+    out_ref[...] = projected.astype(out_ref.dtype)
+    for copy in picks + backs + sent + [across, beside, onward]:
+        copy.wait_send()
+
+
+def per_device_fused(query, key, value, middle_offsets, upper_offsets, out_weight):
+    rows, width = query.shape
+    seq_total = lax.axis_size("seq")
+    heads = width // HD
+    pairs = 2 * heads
+    taken = rows // MIDDLE_DILATION
+    whole = pl.BlockSpec(memory_space=pltpu.VMEM)
+    scalars = pl.BlockSpec(memory_space=pltpu.SMEM)
+    dma = pltpu.SemaphoreType.DMA
+    return pl.pallas_call(
+        functools.partial(fused_kernel, seq_total),
+        out_shape=jax.ShapeDtypeStruct((rows // 4, out_weight.shape[1]), jnp.bfloat16),
+        in_specs=[whole, whole, whole, scalars, scalars, whole],
+        out_specs=whole,
+        scratch_shapes=[
+            pltpu.VMEM((pairs, taken, rows), jnp.bfloat16),
+            pltpu.VMEM((pairs, 3 * HD, taken), jnp.bfloat16),
+            pltpu.VMEM((seq_total, 3 * HD, taken), jnp.bfloat16),
+            pltpu.VMEM((seq_total, HD + STAT_ROWS, taken), jnp.bfloat16),
+            pltpu.VMEM((pairs, HD + STAT_ROWS, taken), jnp.bfloat16),
+            pltpu.VMEM((heads, HD, rows), jnp.float32),
+            pltpu.VMEM((heads, 8, rows), jnp.float32),
+            pltpu.VMEM((4, width, taken), jnp.bfloat16),
+            pltpu.VMEM((4, width, taken), jnp.bfloat16),
+            pltpu.VMEM((4,) + out_weight.shape, jnp.bfloat16),
+            dma((seq_total,)),
+            dma((seq_total,)),
+            dma((seq_total,)),
+            dma((seq_total,)),
+            dma((4,)),
+            dma((4,)),
+            dma((4,)),
+            dma((4,)),
+        ],
+        compiler_params=pltpu.CompilerParams(
+            collective_id=0, has_side_effects=True, vmem_limit_bytes=48 * 2**20
+        ),
+    )(query, key, value, middle_offsets, upper_offsets, out_weight)
+
+
 def solution(mesh):
     in_specs = (
         P("seq", "head"),
@@ -157,6 +452,8 @@
         P("head", None),
     )
     out_specs = P(("seq", "head"), None)
+    seq_total, head_shards = mesh.shape["seq"], mesh.shape["head"]
+    one_segment = seq_total == SPAN and seq_total // 2 == MIDDLE_DILATION and head_shards == 4
     return jax.shard_map(
-        per_device, mesh=mesh, in_specs=in_specs, out_specs=out_specs, check_vma=False
-    )
+        per_device_fused if one_segment else per_device, mesh=mesh, in_specs=in_specs, out_specs=out_specs, check_vma=False
+    )

time: 165 us -> 35.4 us (0.21)
  blocking collectives: 55.6 us -> 0 us
  waiting for transfers between devices: 51.2 us -> 0 us
  Pallas kernels: 0 us -> 29.2 us
  between operations: 13.7 us -> 0.02 us
  local copies, waits for them, and re-layouts: 19.3 us -> 5.9 us
  other arithmetic: 12.1 us -> 0 us
  matrix products: 8.54 us -> 0 us
  starting transfers between devices: 3.61 us -> 0 us
    all_gather x2 -> x0, blocking collectives: 55.6 us -> none  [the longest x1 28.2 us: per_device(): lax.all_gather(top_key_local, 'seq', axis=0, tiled=True)]
    pallas_call x0 -> x1, Pallas kernels: none -> 29.2 us  [per_device_fused(): pl.pallas_call(functools.partial(fused_kernel, seq_total), out_shape=jax....]
    reduce_scatter x1 -> x0, waiting for transfers between devices: 28.9 us -> none  [per_device(): lax.psum_scatter(jnp.dot(attention, out_weight, preferred_element_type=jn...]
    ppermute x3 -> x0, waiting for transfers between devices: 22.2 us -> none  [partner_2(): return lax.ppermute(value, axis, pairs)]
    select_n x12 -> x0, local copies, waits for them, and re-layouts: 12.2 us -> none  [scatter_rows(): spread_out = jnp.where(chosen[None], values[:, None], filler)]
    dot_general x7 -> x0, matrix products: 8.54 us -> none  [the longest x3 3.67 us: attend_segment(): jnp.einsum('qhd,khd->hqk', query_matrix_rows, key_matrix_rows, preferred_...]
    reduce_sum x4 -> x0, other arithmetic: 6.69 us -> none  [the longest x3 4.04 us: attend_segment(): total = jnp.sum(mass, axis=2)]
    unnamed x23 -> x13, local copies, waits for them, and re-layouts: 1.03 us -> 5.9 us
  transfers between devices with their start and end apart: 4 -> 0, of which waited for: 3 -> 0; matrix products, arithmetic and copies ran while one was open for 8% -> 0% of each run, Pallas kernels for 0% -> 0%
where the time goes in v1:
time: 35.4 us; the launch traced here: 35.1 us
  Pallas kernels  29.2 us (82%)
  local copies, waits for them, and re-layouts  5.9 us (17%)
    pallas_call x1, Pallas kernels, per_device_fused(): pl.pallas_call(functools.partial(fused_kernel, seq_total), out_shape=jax....  29.2 us
    unnamed x13, local copies, waits for them, and re-layouts  5.9 us

profile of v1, /device:TPU:0, one launch (start us, length us, event | category | flops | bytes accessed | tf_op | source)
XLA Modules:
  0.0 35.1 jit_solution(11570527272918190814)
XLA Ops:
  0.0 0.0 copy-start
  0.0 1.0 %copy-done = bf16[256,1024]{1,0:T(8,128)(2,1)S(1)} copy-done((bf16[256,1024]{1,0:T(8,128)(2,1)S(1)}, bf16[256,1024]{1,0:T(8,128)(2,1)}, u32[]{:S(2)}) %copy-start) | copy-done | bytes 524312
  1.0 0.0 copy-start.1
  1.0 0.9 %copy-done.1 = bf16[512,256]{1,0:T(8,128)(2,1)S(1)} copy-done((bf16[512,256]{1,0:T(8,128)(2,1)S(1)}, bf16[512,256]{1,0:T(8,128)(2,1)}, u32[]{:S(2)}) %copy-start.1) | copy-done | bytes 262168
  2.0 0.0 copy-start.2
  2.0 0.9 %copy-done.2 = bf16[512,256]{1,0:T(8,128)(2,1)S(1)} copy-done((bf16[512,256]{1,0:T(8,128)(2,1)S(1)}, bf16[512,256]{1,0:T(8,128)(2,1)}, u32[]{:S(2)}) %copy-start.2) | copy-done | bytes 262168
  2.9 0.0 copy-start.3
  2.9 0.9 %copy-done.3 = bf16[512,256]{1,0:T(8,128)(2,1)S(1)} copy-done((bf16[512,256]{1,0:T(8,128)(2,1)S(1)}, bf16[512,256]{1,0:T(8,128)(2,1)}, u32[]{:S(2)}) %copy-start.3) | copy-done | bytes 262168
  3.9 0.0 copy-start.4
  3.9 0.7 %copy-done.4 = s32[4]{0:T(128)S(1)} copy-done((s32[4]{0:T(128)S(1)}, s32[4]{0:T(128)}, u32[]{:S(2)}) %copy-start.4) | copy-done | bytes 40
  4.5 0.0 copy-start.5
  4.6 0.7 %copy-done.5 = s32[4]{0:T(128)S(1)} copy-done((s32[4]{0:T(128)S(1)}, s32[4]{0:T(128)}, u32[]{:S(2)}) %copy-start.5) | copy-done | bytes 40
  5.2 29.2 %shard_map.64 = bf16[128,1024]{1,0:T(8,128)(2,1)S(1)} custom-call(bf16[512,256]{1,0:T(8,128)(2,1)S(1)} %copy-done.1, bf16[512,256]{1,0:T(8,128)(2,1)S(1)} %copy-done.2, bf16[512,256]{1,0:T(8,128)(2,1)S(1)} %copy-done.3, s32[4]{0:T(128)S(1)} %copy-done.4, s32[4]{0:T(128)S(1)} %copy-done.5, bf16[256,1024]{1,0:T(8,128)(2,1)S(1)} %copy-done), custom_call_target="tpu_custom_call" | custom-call | tf_op jit(solution)/shard_map/pallas_call | solution.py:414
  34.4 0.7 %copy.8 = bf16[128,1024]{1,0:T(8,128)(2,1)} copy(bf16[128,1024]{1,0:T(8,128)(2,1)S(1)} %shard_map.64) | data formatting | bytes 524288
Async XLA Ops:
  0.0 1.0 %copy-start = (bf16[256,1024]{1,0:T(8,128)(2,1)S(1)}, bf16[256,1024]{1,0:T(8,128)(2,1)}, u32[]{:S(2)}) copy-start(bf16[256,1024]{1,0:T(8,128)(2,1)} %weight_ref.1) | copy-start | bytes 1572868
  1.0 0.9 %copy-start.1 = (bf16[512,256]{1,0:T(8,128)(2,1)S(1)}, bf16[512,256]{1,0:T(8,128)(2,1)}, u32[]{:S(2)}) copy-start(bf16[512,256]{1,0:T(8,128)(2,1)} %query_ref.1) | copy-start | bytes 786436
  2.0 0.9 %copy-start.2 = (bf16[512,256]{1,0:T(8,128)(2,1)S(1)}, bf16[512,256]{1,0:T(8,128)(2,1)}, u32[]{:S(2)}) copy-start(bf16[512,256]{1,0:T(8,128)(2,1)} %key_ref.1) | copy-start | bytes 786436
  2.9 0.9 %copy-start.3 = (bf16[512,256]{1,0:T(8,128)(2,1)S(1)}, bf16[512,256]{1,0:T(8,128)(2,1)}, u32[]{:S(2)}) copy-start(bf16[512,256]{1,0:T(8,128)(2,1)} %value_ref.1) | copy-start | bytes 786436
  3.9 0.7 %copy-start.4 = (s32[4]{0:T(128)S(1)}, s32[4]{0:T(128)}, u32[]{:S(2)}) copy-start(s32[4]{0:T(128)} %middle_ref.1) | copy-start | bytes 52
  4.5 0.7 %copy-start.5 = (s32[4]{0:T(128)S(1)}, s32[4]{0:T(128)}, u32[]{:S(2)}) copy-start(s32[4]{0:T(128)} %upper_ref.1) | copy-start | bytes 52

commit v2 on v1

--- a/solution.py
+++ b/solution.py
@@ -168,13 +168,20 @@
 
 def fused_kernel(
     seq_total,
+    query_hbm,
+    key_hbm,
+    value_hbm,
+    middle_hbm,
+    upper_hbm,
+    weight_hbm,
+    out_ref,
     query_ref,
     key_ref,
     value_ref,
     middle_ref,
     upper_ref,
     weight_ref,
-    out_ref,
+    load,
     select,
     message,
     got,
@@ -204,8 +211,23 @@
     ]
     rows = query_ref.shape[0]
     heads = query_ref.shape[1] // HD
+    half, place = lax.div(seq, heads), lax.rem(seq, heads)
     taken = rows // MIDDLE_DILATION
     offset_refs = (middle_ref, upper_ref)
+
+    loads = []
+    for i, (source, target) in enumerate(
+        (
+            (middle_hbm, middle_ref),
+            (upper_hbm, upper_ref),
+            (query_hbm, query_ref),
+            (value_hbm, value_ref),
+            (key_hbm, key_ref),
+            (weight_hbm, weight_ref),
+        )
+    ):
+        loads.append(pltpu.make_async_copy(source, target, load.at[i]))
+        loads[-1].start()
 
     barrier = pltpu.get_barrier_semaphore()
     for step in range(1, seq_total):
@@ -220,47 +242,78 @@
             barrier, inc=1, device_id=(seq, peers[step]), device_id_type=MESH
         )
 
+    for copy in loads[:5]:
+        copy.wait()
     query_t = (query_ref[...] * jnp.bfloat16(HD**-0.5)).T
     value_t = value_ref[...].T
     distance = lax.broadcasted_iota(jnp.int32, (taken, rows), 1) - MIDDLE_DILATION * (
         lax.broadcasted_iota(jnp.int32, (taken, rows), 0)
     )
-    for level in range(2):
-        for one in range(heads):
-            pair = level * heads + one
-            span = slice(one * HD, (one + 1) * HD)
-            chosen = jnp.where(
+    near, far = [], []
+
+    def pick(one):
+        span = slice(one * HD, (one + 1) * HD)
+        for level in range(2):
+            select[one, level * taken : (level + 1) * taken] = jnp.where(
                 distance == offset_refs[level][one], jnp.float32(1), jnp.float32(0)
             ).astype(jnp.bfloat16)
-            select[pair] = chosen
-            both_t = jnp.concatenate([query_t[span], value_t[span]], axis=0)
-            message[pair, 0 : 2 * HD] = lax.dot_general(
-                both_t,
-                chosen,
-                (((1,), (1,)), ((), ())),
-                preferred_element_type=jnp.float32,
-            ).astype(jnp.bfloat16)
-            picked = dot_f32(chosen, key_ref[:, span])
-            message[pair, 2 * HD : 3 * HD] = jnp.concatenate(
-                [picked[: taken // 2], picked[taken // 2 :]], axis=1
-            ).astype(jnp.bfloat16)
-
+        chosen = select[one]
+        both_t = lax.dot_general(
+            jnp.concatenate([value_t[span], query_t[span]], axis=0),
+            chosen,
+            (((1,), (1,)), ((), ())),
+            preferred_element_type=jnp.float32,
+        ).astype(jnp.bfloat16)
+        picked = dot_f32(chosen, key_ref[:, span]).astype(jnp.bfloat16)
+        for level in range(2):
+            lanes = slice(level * taken, (level + 1) * taken)
+            first = 2 * HD * level
+            message[one, first : first + HD] = both_t[:HD, lanes]
+            message[one, first + HD : first + 2 * HD] = jnp.concatenate(
+                [
+                    picked[level * taken : level * taken + taken // 2],
+                    picked[level * taken + taken // 2 : (level + 1) * taken],
+                ],
+                axis=1,
+            )
+            message[one, (4 + level) * HD : (5 + level) * HD] = both_t[HD:, lanes]
+
+    def send_picked(one):
+        slot = lax.rem(one - place + heads, heads)
+        far.append(
+            pltpu.make_async_remote_copy(
+                src_ref=message.at[one, 0 : 4 * HD],
+                dst_ref=got.at[heads + slot, 0 : 4 * HD],
+                send_sem=send_pick.at[heads + one],
+                recv_sem=recv_pick.at[heads + slot],
+                device_id=((1 - half) * heads + one, head),
+                device_id_type=MESH,
+            )
+        )
+        far[-1].start()
+        near.append(
+            pltpu.make_async_remote_copy(
+                src_ref=message.at[one],
+                dst_ref=got.at[slot],
+                send_sem=send_pick.at[one],
+                recv_sem=recv_pick.at[slot],
+                device_id=(half * heads + one, head),
+                device_id_type=MESH,
+            )
+        )
+        pl.when(one != place)(near[-1].start)
+
+    for one in range(heads // 2):
+        pick(one)
     pl.semaphore_wait(barrier, seq_total + 2)
-    picks = []
-    for step in range(1, seq_total):
-        target = lax.rem(seq + step, seq_total)
-        picks.append(
-            pltpu.make_async_remote_copy(
-                src_ref=message.at[target],
-                dst_ref=got.at[step],
-                send_sem=send_pick.at[step],
-                recv_sem=recv_pick.at[step],
-                device_id=(target, head),
-                device_id_type=MESH,
-            )
-        )
-        picks[-1].start()
-    got[0] = message[seq]
+    for one in range(heads // 2):
+        send_picked(one)
+    for one in range(heads // 2, heads):
+        pick(one)
+    for one in range(heads // 2, heads):
+        send_picked(one)
+    got[0] = message[place]
+    loads[5].wait()
 
     def weight_copy(source, slot, peer):
         return pltpu.make_async_remote_copy(
@@ -277,11 +330,11 @@
     beside = weight_copy(weight_ref, 1, 1)
     beside.start()
 
-    half = rows // 2
+    cut = rows // 2
     for one in range(heads):
         span = slice(one * HD, (one + 1) * HD)
         for part in range(2):
-            lanes = slice(part * half, (part + 1) * half)
+            lanes = slice(part * cut, (part + 1) * cut)
             scores = dot_f32(key_ref[:, span], query_t[span, lanes])
             row_max = jnp.max(scores, axis=0, keepdims=True)
             mass = jnp.exp(scores - row_max)
@@ -289,49 +342,64 @@
             bottom_stats[one, 1:2, lanes] = jnp.sum(mass, axis=0, keepdims=True)
             bottom[one, :, lanes] = dot_f32(value_t[span], mass.astype(jnp.bfloat16))
 
-    for copy in picks:
-        copy.wait_recv()
-    keys = jnp.concatenate([got[i, 2 * HD : 3 * HD] for i in range(seq_total)], axis=0)
-    values_t = jnp.concatenate([got[i, HD : 2 * HD] for i in range(seq_total)], axis=1)
+    for slot in range(1, 2 * heads):
+        deep = 6 * HD if slot < heads else 4 * HD
+        pltpu.make_async_remote_copy(
+            src_ref=message.at[0, 0:deep],
+            dst_ref=got.at[slot, 0:deep],
+            send_sem=send_pick.at[slot],
+            recv_sem=recv_pick.at[slot],
+            device_id=(lax.rem(seq + 1, seq_total), head),
+            device_id_type=MESH,
+        ).wait_recv()
+
     backs = []
-    for part in range(seq_total // 2):
-        block = jnp.concatenate(
-            [got[2 * part, 0:HD], got[2 * part + 1, 0:HD]], axis=1
-        )
-        blank = jnp.zeros_like(block)
-        first = dot_f32(keys, jnp.concatenate([block, blank], axis=0))
-        second = dot_f32(keys, jnp.concatenate([blank, block], axis=0))
-        row_max = jnp.maximum(
-            jnp.max(first, axis=0, keepdims=True), jnp.max(second, axis=0, keepdims=True)
-        )
-        first = jnp.exp(first - row_max)
-        second = jnp.exp(second - row_max)
-        total = jnp.sum(first, axis=0, keepdims=True) + jnp.sum(
-            second, axis=0, keepdims=True
-        )
-        first = first.astype(jnp.bfloat16)
-        second = second.astype(jnp.bfloat16)
-        pieces = []
-        for i in range(seq_total):
-            pieces.append(first[i * HD : (i + 1) * HD])
-            pieces.append(second[i * HD : (i + 1) * HD])
-        weighted = dot_f32(values_t, jnp.concatenate(pieces, axis=0))
-        stats = three_parts(row_max) + three_parts(total)
+    for slots in ((1, 2), (3, 0)):
+        weighted, stats = [], []
+        for level in range(2):
+            first = 2 * HD * level
+            values_t = jnp.concatenate(
+                [got[i, first : first + HD] for i in range(seq_total)], axis=1
+            )
+            keys = jnp.concatenate(
+                [got[i, first + HD : first + 2 * HD] for i in range(seq_total)], axis=0
+            )
+            block = jnp.concatenate(
+                [got[i, (4 + level) * HD : (5 + level) * HD] for i in slots], axis=1
+            )
+            blank = jnp.zeros_like(block)
+            left = dot_f32(keys, jnp.concatenate([block, blank], axis=0))
+            right = dot_f32(keys, jnp.concatenate([blank, block], axis=0))
+            row_max = jnp.maximum(
+                jnp.max(left, axis=0, keepdims=True), jnp.max(right, axis=0, keepdims=True)
+            )
+            left = jnp.exp(left - row_max)
+            right = jnp.exp(right - row_max)
+            total = jnp.sum(left, axis=0, keepdims=True) + jnp.sum(
+                right, axis=0, keepdims=True
+            )
+            left = left.astype(jnp.bfloat16)
+            right = right.astype(jnp.bfloat16)
+            pieces = []
+            for i in range(seq_total):
+                pieces.append(left[i * HD : (i + 1) * HD])
+                pieces.append(right[i * HD : (i + 1) * HD])
+            weighted.append(dot_f32(values_t, jnp.concatenate(pieces, axis=0)))
+            stats += three_parts(row_max) + three_parts(total)
         stats.append(jnp.zeros((STAT_ROWS - len(stats), 2 * taken), jnp.float32))
-        packed = jnp.concatenate([weighted] + stats, axis=0).astype(jnp.bfloat16)
-        for step in (2 * part, 2 * part + 1):
-            begin = (step - 2 * part) * taken
+        packed = jnp.concatenate(weighted + stats, axis=0).astype(jnp.bfloat16)
+        for step, begin in zip(slots, (0, taken)):
+            if step == 0:
+                returned[place] = packed[:, begin : begin + taken]
+                continue
             result[step] = packed[:, begin : begin + taken]
-            if step == 0:
-                returned[seq] = packed[:, begin : begin + taken]
-                continue
             backs.append(
                 pltpu.make_async_remote_copy(
                     src_ref=result.at[step],
-                    dst_ref=returned.at[seq],
+                    dst_ref=returned.at[place],
                     send_sem=send_back.at[step],
                     recv_sem=recv_back.at[step],
-                    device_id=(lax.rem(seq - step + seq_total, seq_total), head),
+                    device_id=(half * heads + lax.rem(place - step + heads, heads), head),
                     device_id_type=MESH,
                 )
             )
@@ -341,13 +409,14 @@
     onward = weight_copy(weights_got.at[2], 3, 1)
     onward.start()
 
-    for step in range(1, seq_total):
+    for step in range(1, heads):
+        source = lax.rem(place + step, heads)
         pltpu.make_async_remote_copy(
             src_ref=result.at[step],
-            dst_ref=returned.at[lax.rem(seq + step, seq_total)],
+            dst_ref=returned.at[source],
             send_sem=send_back.at[step],
             recv_sem=recv_back.at[step],
-            device_id=(lax.rem(seq + step, seq_total), head),
+            device_id=(half * heads + source, head),
             device_id_type=MESH,
         ).wait_recv()
     residue = lax.rem(lax.broadcasted_iota(jnp.int32, (1, rows), 1), MIDDLE_DILATION)
@@ -356,16 +425,15 @@
         totals = [bottom_stats[one, 1:2]]
         sums = [bottom[one]]
         for level in range(2):
-            pair = level * heads + one
-            spread = dot_f32(returned[pair], select[pair])
-            row_max = spread[HD : HD + 1] + spread[HD + 1 : HD + 2] + spread[HD + 2 : HD + 3]
+            lines = slice(level * taken, (level + 1) * taken)
+            spread = dot_f32(returned[one, level * HD : (level + 1) * HD], select[one, lines])
+            stats = dot_f32(returned[one, 2 * HD :], select[one, lines])[6 * level :]
+            row_max = stats[0:1] + stats[1:2] + stats[2:3]
             maxima.append(
                 jnp.where(residue == offset_refs[level][one], row_max, -jnp.inf)
             )
-            totals.append(
-                spread[HD + 3 : HD + 4] + spread[HD + 4 : HD + 5] + spread[HD + 5 : HD + 6]
-            )
-            sums.append(spread[0:HD])
+            totals.append(stats[3:4] + stats[4:5] + stats[5:6])
+            sums.append(spread)
         highest = jnp.maximum(jnp.maximum(maxima[0], maxima[1]), maxima[2])
         factors = [jnp.exp(row_max - highest) for row_max in maxima]
         denominator = sum(f * t for f, t in zip(factors, totals))
@@ -398,7 +466,9 @@
         sent[step - 1].wait_recv()
         projected += dot_f32(columns_got[step].T, weights_got[step])
     out_ref[...] = projected.astype(out_ref.dtype)
-    for copy in picks + backs + sent + [across, beside, onward]:
+    for one in range(heads):
+        pl.when(one != place)(near[one].wait_send)
+    for copy in far + backs + sent + [across, beside, onward]:
         copy.wait_send()
 
 
@@ -406,22 +476,28 @@
     rows, width = query.shape
     seq_total = lax.axis_size("seq")
     heads = width // HD
-    pairs = 2 * heads
     taken = rows // MIDDLE_DILATION
     whole = pl.BlockSpec(memory_space=pltpu.VMEM)
-    scalars = pl.BlockSpec(memory_space=pltpu.SMEM)
+    anywhere = pl.BlockSpec(memory_space=pl.ANY)
     dma = pltpu.SemaphoreType.DMA
     return pl.pallas_call(
         functools.partial(fused_kernel, seq_total),
         out_shape=jax.ShapeDtypeStruct((rows // 4, out_weight.shape[1]), jnp.bfloat16),
-        in_specs=[whole, whole, whole, scalars, scalars, whole],
+        in_specs=[anywhere] * 6,
         out_specs=whole,
         scratch_shapes=[
-            pltpu.VMEM((pairs, taken, rows), jnp.bfloat16),
-            pltpu.VMEM((pairs, 3 * HD, taken), jnp.bfloat16),
-            pltpu.VMEM((seq_total, 3 * HD, taken), jnp.bfloat16),
-            pltpu.VMEM((seq_total, HD + STAT_ROWS, taken), jnp.bfloat16),
-            pltpu.VMEM((pairs, HD + STAT_ROWS, taken), jnp.bfloat16),
+            pltpu.VMEM(query.shape, query.dtype),
+            pltpu.VMEM(key.shape, key.dtype),
+            pltpu.VMEM(value.shape, value.dtype),
+            pltpu.SMEM(middle_offsets.shape, jnp.int32),
+            pltpu.SMEM(upper_offsets.shape, jnp.int32),
+            pltpu.VMEM(out_weight.shape, out_weight.dtype),
+            dma((6,)),
+            pltpu.VMEM((heads, 2 * taken, rows), jnp.bfloat16),
+            pltpu.VMEM((heads, 6 * HD, taken), jnp.bfloat16),
+            pltpu.VMEM((seq_total, 6 * HD, taken), jnp.bfloat16),
+            pltpu.VMEM((heads, 2 * HD + STAT_ROWS, taken), jnp.bfloat16),
+            pltpu.VMEM((heads, 2 * HD + STAT_ROWS, taken), jnp.bfloat16),
             pltpu.VMEM((heads, HD, rows), jnp.float32),
             pltpu.VMEM((heads, 8, rows), jnp.float32),
             pltpu.VMEM((4, width, taken), jnp.bfloat16),
@@ -437,7 +513,7 @@
             dma((4,)),
         ],
         compiler_params=pltpu.CompilerParams(
-            collective_id=0, has_side_effects=True, vmem_limit_bytes=48 * 2**20
+            collective_id=0, has_side_effects=True, vmem_limit_bytes=60 * 2**20
         ),
     )(query, key, value, middle_offsets, upper_offsets, out_weight)
 

time: 35.4 us -> 33.2 us (0.938)
  local copies, waits for them, and re-layouts: 5.9 us -> 1.67 us
  Pallas kernels: 29.2 us -> 31.4 us
    unnamed x13 -> x1, local copies, waits for them, and re-layouts: 5.9 us -> 1.67 us
    pallas_call x1, Pallas kernels: 29.2 us -> 31.4 us  [per_device_fused(): pl.pallas_call(functools.partial(fused_kernel, seq_total), out_shape=jax....]
where the time goes in v2:
time: 33.2 us; the launch traced here: 33.1 us
  Pallas kernels  31.4 us (95%)
  local copies, waits for them, and re-layouts  1.67 us (5%)
    pallas_call x1, Pallas kernels, per_device_fused(): pl.pallas_call(functools.partial(fused_kernel, seq_total), out_shape=jax....  31.4 us
    unnamed x1, local copies, waits for them, and re-layouts  1.67 us

profile of v2, /device:TPU:0, one launch (start us, length us, event | category | flops | bytes accessed | tf_op | source)
XLA Modules:
  0.0 33.1 jit_solution(11332653123314568138)
XLA Ops:
  0.0 31.4 %shard_map.64 = bf16[128,1024]{1,0:T(8,128)(2,1)} custom-call(bf16[512,256]{1,0:T(8,128)(2,1)} %query_hbm.1, bf16[512,256]{1,0:T(8,128)(2,1)} %key_hbm.1, bf16[512,256]{1,0:T(8,128)(2,1)} %value_hbm.1, s32[4]{0:T(128)} %middle_hbm.1, s32[4]{0:T(128)} %upper_hbm.1, bf16[256,1024]{1,0:T(8,128)(2,1)} %weight_hbm.1), custom_call_target="tpu_custom_call" | custom-call | tf_op jit(solution)/shard_map/pallas_call | solution.py:483
  31.4 1.7 %copy.8 = bf16[128,1024]{1,0:T(8,128)(2,1)} copy(bf16[128,1024]{1,0:T(8,128)(2,1)} %shard_map.64) | data formatting | bytes 524288

commit v3 on v1

--- a/solution.py
+++ b/solution.py
@@ -168,13 +168,20 @@
 
 def fused_kernel(
     seq_total,
+    query_hbm,
+    key_hbm,
+    value_hbm,
+    middle_hbm,
+    upper_hbm,
+    weight_hbm,
+    out_ref,
     query_ref,
     key_ref,
     value_ref,
     middle_ref,
     upper_ref,
     weight_ref,
-    out_ref,
+    load,
     select,
     message,
     got,
@@ -207,6 +214,20 @@
     taken = rows // MIDDLE_DILATION
     offset_refs = (middle_ref, upper_ref)
 
+    loads = []
+    for i, (source, target) in enumerate(
+        (
+            (middle_hbm, middle_ref),
+            (upper_hbm, upper_ref),
+            (query_hbm, query_ref),
+            (value_hbm, value_ref),
+            (key_hbm, key_ref),
+            (weight_hbm, weight_ref),
+        )
+    ):
+        loads.append(pltpu.make_async_copy(source, target, load.at[i]))
+        loads[-1].start()
+
     barrier = pltpu.get_barrier_semaphore()
     for step in range(1, seq_total):
         pl.semaphore_signal(
@@ -220,20 +241,24 @@
             barrier, inc=1, device_id=(seq, peers[step]), device_id_type=MESH
         )
 
+    for copy in loads[:5]:
+        copy.wait()
     query_t = (query_ref[...] * jnp.bfloat16(HD**-0.5)).T
     value_t = value_ref[...].T
     distance = lax.broadcasted_iota(jnp.int32, (taken, rows), 1) - MIDDLE_DILATION * (
         lax.broadcasted_iota(jnp.int32, (taken, rows), 0)
     )
-    for level in range(2):
-        for one in range(heads):
+    picks = {}
+
+    def pick(one):
+        span = slice(one * HD, (one + 1) * HD)
+        both_t = jnp.concatenate([query_t[span], value_t[span]], axis=0)
+        for level in range(2):
             pair = level * heads + one
-            span = slice(one * HD, (one + 1) * HD)
             chosen = jnp.where(
                 distance == offset_refs[level][one], jnp.float32(1), jnp.float32(0)
             ).astype(jnp.bfloat16)
             select[pair] = chosen
-            both_t = jnp.concatenate([query_t[span], value_t[span]], axis=0)
             message[pair, 0 : 2 * HD] = lax.dot_general(
                 both_t,
                 chosen,
@@ -245,22 +270,29 @@
                 [picked[: taken // 2], picked[taken // 2 :]], axis=1
             ).astype(jnp.bfloat16)
 
-    pl.semaphore_wait(barrier, seq_total + 2)
-    picks = []
-    for step in range(1, seq_total):
-        target = lax.rem(seq + step, seq_total)
-        picks.append(
-            pltpu.make_async_remote_copy(
-                src_ref=message.at[target],
-                dst_ref=got.at[step],
-                send_sem=send_pick.at[step],
-                recv_sem=recv_pick.at[step],
-                device_id=(target, head),
-                device_id_type=MESH,
-            )
-        )
-        picks[-1].start()
+    def send_picked(pair):
+        slot = lax.rem(pair - seq + seq_total, seq_total)
+        picks[pair] = pltpu.make_async_remote_copy(
+            src_ref=message.at[pair],
+            dst_ref=got.at[slot],
+            send_sem=send_pick.at[pair],
+            recv_sem=recv_pick.at[slot],
+            device_id=(pair, head),
+            device_id_type=MESH,
+        )
+        pl.when(pair != seq)(picks[pair].start)
+
+    for begin in range(0, heads, 2):
+        for one in (begin, begin + 1):
+            pick(one)
+        if begin == 0:
+            pl.semaphore_wait(barrier, seq_total + 2)
+        for one in (begin, begin + 1):
+            for level in range(2):
+                send_picked(level * heads + one)
     got[0] = message[seq]
+
+    loads[5].wait()
 
     def weight_copy(source, slot, peer):
         return pltpu.make_async_remote_copy(
@@ -289,15 +321,22 @@
             bottom_stats[one, 1:2, lanes] = jnp.sum(mass, axis=0, keepdims=True)
             bottom[one, :, lanes] = dot_f32(value_t[span], mass.astype(jnp.bfloat16))
 
-    for copy in picks:
-        copy.wait_recv()
+    for slot in range(1, seq_total):
+        pltpu.make_async_remote_copy(
+            src_ref=message.at[0],
+            dst_ref=got.at[slot],
+            send_sem=send_pick.at[0],
+            recv_sem=recv_pick.at[slot],
+            device_id=(lax.rem(seq + 1, seq_total), head),
+            device_id_type=MESH,
+        ).wait_recv()
     keys = jnp.concatenate([got[i, 2 * HD : 3 * HD] for i in range(seq_total)], axis=0)
     values_t = jnp.concatenate([got[i, HD : 2 * HD] for i in range(seq_total)], axis=1)
     backs = []
-    for part in range(seq_total // 2):
-        block = jnp.concatenate(
-            [got[2 * part, 0:HD], got[2 * part + 1, 0:HD]], axis=1
-        )
+    middle = seq_total // 2
+    for i in range(middle):
+        slots = (middle - i, (middle + 1 + i) % seq_total)
+        block = jnp.concatenate([got[slot, 0:HD] for slot in slots], axis=1)
         blank = jnp.zeros_like(block)
         first = dot_f32(keys, jnp.concatenate([block, blank], axis=0))
         second = dot_f32(keys, jnp.concatenate([blank, block], axis=0))
@@ -319,8 +358,7 @@
         stats = three_parts(row_max) + three_parts(total)
         stats.append(jnp.zeros((STAT_ROWS - len(stats), 2 * taken), jnp.float32))
         packed = jnp.concatenate([weighted] + stats, axis=0).astype(jnp.bfloat16)
-        for step in (2 * part, 2 * part + 1):
-            begin = (step - 2 * part) * taken
+        for step, begin in zip(slots, (0, taken)):
             result[step] = packed[:, begin : begin + taken]
             if step == 0:
                 returned[seq] = packed[:, begin : begin + taken]
@@ -398,7 +436,9 @@
         sent[step - 1].wait_recv()
         projected += dot_f32(columns_got[step].T, weights_got[step])
     out_ref[...] = projected.astype(out_ref.dtype)
-    for copy in picks + backs + sent + [across, beside, onward]:
+    for pair in range(seq_total):
+        pl.when(pair != seq)(picks[pair].wait_send)
+    for copy in backs + sent + [across, beside, onward]:
         copy.wait_send()
 
 
@@ -409,14 +449,21 @@
     pairs = 2 * heads
     taken = rows // MIDDLE_DILATION
     whole = pl.BlockSpec(memory_space=pltpu.VMEM)
-    scalars = pl.BlockSpec(memory_space=pltpu.SMEM)
+    anywhere = pl.BlockSpec(memory_space=pl.ANY)
     dma = pltpu.SemaphoreType.DMA
     return pl.pallas_call(
         functools.partial(fused_kernel, seq_total),
         out_shape=jax.ShapeDtypeStruct((rows // 4, out_weight.shape[1]), jnp.bfloat16),
-        in_specs=[whole, whole, whole, scalars, scalars, whole],
+        in_specs=[anywhere] * 6,
         out_specs=whole,
         scratch_shapes=[
+            pltpu.VMEM(query.shape, query.dtype),
+            pltpu.VMEM(key.shape, key.dtype),
+            pltpu.VMEM(value.shape, value.dtype),
+            pltpu.SMEM(middle_offsets.shape, jnp.int32),
+            pltpu.SMEM(upper_offsets.shape, jnp.int32),
+            pltpu.VMEM(out_weight.shape, out_weight.dtype),
+            dma((6,)),
             pltpu.VMEM((pairs, taken, rows), jnp.bfloat16),
             pltpu.VMEM((pairs, 3 * HD, taken), jnp.bfloat16),
             pltpu.VMEM((seq_total, 3 * HD, taken), jnp.bfloat16),
@@ -437,7 +484,7 @@
             dma((4,)),
         ],
         compiler_params=pltpu.CompilerParams(
-            collective_id=0, has_side_effects=True, vmem_limit_bytes=48 * 2**20
+            collective_id=0, has_side_effects=True, vmem_limit_bytes=60 * 2**20
         ),
     )(query, key, value, middle_offsets, upper_offsets, out_weight)
 

time: 35.4 us -> 30.6 us (0.86)
  local copies, waits for them, and re-layouts: 5.9 us -> 1.67 us
  Pallas kernels: 29.2 us -> 28.8 us
    unnamed x13 -> x1, local copies, waits for them, and re-layouts: 5.9 us -> 1.67 us
    pallas_call x1, Pallas kernels: 29.2 us -> 28.8 us  [per_device_fused(): pl.pallas_call(functools.partial(fused_kernel, seq_total), out_shape=jax....]
where the time goes in v3:
time: 30.6 us; the launch traced here: 30.4 us
  Pallas kernels  28.8 us (94%)
  local copies, waits for them, and re-layouts  1.67 us (5%)
    pallas_call x1, Pallas kernels, per_device_fused(): pl.pallas_call(functools.partial(fused_kernel, seq_total), out_shape=jax....  28.8 us
    unnamed x1, local copies, waits for them, and re-layouts  1.67 us

profile of v3, /device:TPU:0, one launch (start us, length us, event | category | flops | bytes accessed | tf_op | source)
XLA Modules:
  0.0 30.4 jit_solution(11210825721546178153)
XLA Ops:
  0.0 28.8 %shard_map.64 = bf16[128,1024]{1,0:T(8,128)(2,1)} custom-call(bf16[512,256]{1,0:T(8,128)(2,1)} %query_hbm.1, bf16[512,256]{1,0:T(8,128)(2,1)} %key_hbm.1, bf16[512,256]{1,0:T(8,128)(2,1)} %value_hbm.1, s32[4]{0:T(128)} %middle_hbm.1, s32[4]{0:T(128)} %upper_hbm.1, bf16[256,1024]{1,0:T(8,128)(2,1)} %weight_hbm.1), custom_call_target="tpu_custom_call" | custom-call | tf_op jit(solution)/shard_map/pallas_call | solution.py:454
  28.8 1.7 %copy.8 = bf16[128,1024]{1,0:T(8,128)(2,1)} copy(bf16[128,1024]{1,0:T(8,128)(2,1)} %shard_map.64) | data formatting | bytes 524288

commit v4 on v3

--- a/solution.py
+++ b/solution.py
@@ -214,6 +214,19 @@
     taken = rows // MIDDLE_DILATION
     offset_refs = (middle_ref, upper_ref)
 
+    barrier = pltpu.get_barrier_semaphore()
+    for step in range(1, seq_total):
+        pl.semaphore_signal(
+            barrier,
+            inc=1,
+            device_id=(lax.rem(seq + step, seq_total), head),
+            device_id_type=MESH,
+        )
+    for step in range(1, 4):
+        pl.semaphore_signal(
+            barrier, inc=1, device_id=(seq, peers[step]), device_id_type=MESH
+        )
+
     loads = []
     for i, (source, target) in enumerate(
         (
@@ -228,23 +241,10 @@
         loads.append(pltpu.make_async_copy(source, target, load.at[i]))
         loads[-1].start()
 
-    barrier = pltpu.get_barrier_semaphore()
-    for step in range(1, seq_total):
-        pl.semaphore_signal(
-            barrier,
-            inc=1,
-            device_id=(lax.rem(seq + step, seq_total), head),
-            device_id_type=MESH,
-        )
-    for step in range(1, 4):
-        pl.semaphore_signal(
-            barrier, inc=1, device_id=(seq, peers[step]), device_id_type=MESH
-        )
-
     for copy in loads[:5]:
         copy.wait()
-    query_t = (query_ref[...] * jnp.bfloat16(HD**-0.5)).T
-    value_t = value_ref[...].T
+    scale = jnp.bfloat16(HD**-0.5)
+    query_t, value_t = {}, {}
     distance = lax.broadcasted_iota(jnp.int32, (taken, rows), 1) - MIDDLE_DILATION * (
         lax.broadcasted_iota(jnp.int32, (taken, rows), 0)
     )
@@ -252,7 +252,7 @@
 
     def pick(one):
         span = slice(one * HD, (one + 1) * HD)
-        both_t = jnp.concatenate([query_t[span], value_t[span]], axis=0)
+        both_t = jnp.concatenate([query_t[one], value_t[one]], axis=0)
         for level in range(2):
             pair = level * heads + one
             chosen = jnp.where(
@@ -283,11 +283,16 @@
         pl.when(pair != seq)(picks[pair].start)
 
     for begin in range(0, heads, 2):
+        span = slice(begin * HD, (begin + 2) * HD)
+        query_both = (query_ref[:, span] * scale).T
+        value_both = value_ref[:, span].T
+        for i in range(2):
+            query_t[begin + i] = query_both[i * HD : (i + 1) * HD]
+            value_t[begin + i] = value_both[i * HD : (i + 1) * HD]
         for one in (begin, begin + 1):
             pick(one)
-        if begin == 0:
-            pl.semaphore_wait(barrier, seq_total + 2)
-        for one in (begin, begin + 1):
+            if one == 0:
+                pl.semaphore_wait(barrier, seq_total + 2)
             for level in range(2):
                 send_picked(level * heads + one)
     got[0] = message[seq]
@@ -304,22 +309,22 @@
             device_id_type=MESH,
         )
 
-    across = weight_copy(weight_ref, 2, 2)
-    across.start()
-    beside = weight_copy(weight_ref, 1, 1)
-    beside.start()
-
     half = rows // 2
     for one in range(heads):
         span = slice(one * HD, (one + 1) * HD)
         for part in range(2):
             lanes = slice(part * half, (part + 1) * half)
-            scores = dot_f32(key_ref[:, span], query_t[span, lanes])
+            scores = dot_f32(key_ref[:, span], query_t[one][:, lanes])
             row_max = jnp.max(scores, axis=0, keepdims=True)
             mass = jnp.exp(scores - row_max)
             bottom_stats[one, 0:1, lanes] = row_max
             bottom_stats[one, 1:2, lanes] = jnp.sum(mass, axis=0, keepdims=True)
-            bottom[one, :, lanes] = dot_f32(value_t[span], mass.astype(jnp.bfloat16))
+            bottom[one, :, lanes] = dot_f32(value_t[one], mass.astype(jnp.bfloat16))
+
+    across = weight_copy(weight_ref, 2, 2)
+    across.start()
+    beside = weight_copy(weight_ref, 1, 1)
+    beside.start()
 
     for slot in range(1, seq_total):
         pltpu.make_async_remote_copy(
@@ -417,7 +422,7 @@
             ]
 
     sent = []
-    for step in range(1, 4):
+    for step in (2, 3, 1):
         sent.append(
             pltpu.make_async_remote_copy(
                 src_ref=columns.at[peers[step]],
@@ -430,10 +435,14 @@
         )
         sent[-1].start()
     projected = dot_f32(columns[head].T, weight_ref[...])
-    for step, weight in ((1, beside), (2, None), (3, onward)):
+    for step, weight, arriving in (
+        (1, beside, sent[2]),
+        (2, None, sent[0]),
+        (3, onward, sent[1]),
+    ):
         if weight is not None:
             weight.wait_recv()
-        sent[step - 1].wait_recv()
+        arriving.wait_recv()
         projected += dot_f32(columns_got[step].T, weights_got[step])
     out_ref[...] = projected.astype(out_ref.dtype)
     for pair in range(seq_total):

time: 30.6 us -> 30.6 us (level)
  no operation moved by 1% of the time
where the time goes in v4:
time: 30.6 us; the launch traced here: 30.4 us
  Pallas kernels  28.8 us (94%)
  local copies, waits for them, and re-layouts  1.67 us (5%)
    pallas_call x1, Pallas kernels, per_device_fused(): pl.pallas_call(functools.partial(fused_kernel, seq_total), out_shape=jax....  28.8 us
    unnamed x1, local copies, waits for them, and re-layouts  1.67 us

profile of v4, /device:TPU:0, one launch (start us, length us, event | category | flops | bytes accessed | tf_op | source)
XLA Modules:
  0.0 30.4 jit_solution(13766928112737540509)
XLA Ops:
  0.0 28.8 %shard_map.64 = bf16[128,1024]{1,0:T(8,128)(2,1)} custom-call(bf16[512,256]{1,0:T(8,128)(2,1)} %query_hbm.1, bf16[512,256]{1,0:T(8,128)(2,1)} %key_hbm.1, bf16[512,256]{1,0:T(8,128)(2,1)} %value_hbm.1, s32[4]{0:T(128)} %middle_hbm.1, s32[4]{0:T(128)} %upper_hbm.1, bf16[256,1024]{1,0:T(8,128)(2,1)} %weight_hbm.1), custom_call_target="tpu_custom_call" | custom-call | tf_op jit(solution)/shard_map/pallas_call | solution.py:463
  28.8 1.7 %copy.8 = bf16[128,1024]{1,0:T(8,128)(2,1)} copy(bf16[128,1024]{1,0:T(8,128)(2,1)} %shard_map.64) | data formatting | bytes 524288
